TPU v7x, 256 devices: a whole 4x4x8 slice. The times are simulated.
256 devices in a mesh: col: 32 (over z, y), sec: 8 (over x, core).
Axes of the slice: x: 4, y: 4, z: 8, core: 2. Of those that a mesh axis runs over, the one named last changes fastest.
Arguments:
- transfer: float32 [64, 8, 256, 256], P('col', 'sec'), as said below
- hamiltonian: float32 [64, 3, 8, 256, 256], P('col', None, 'sec'), may hold values from -0.375 to 0.375
- kept: int32 [64, 8], P('col', 'sec'), may hold values from 128 to 256, as said below
Outputs:
- left_env: float32 [64, 8, 256, 256], P('col', 'sec')
- energy: float32 [64, 3], P('col')
Inputs may be any that keep to these rules, and one draw needn't show every extreme that they name: Every kept dimension lies between half a sector and a whole sector, and some sector keeps all 256 states. `transfer`: each block is the identity plus an independent normal matrix of entries with deviation 0.2 / sqrt(256).
All inputs are finite; a program needn't handle non-finite values.
Results may differ from a plain program's by a relative error of at most 0.0003.
Values sent between devices are 32-bit elements; how exact they have to be, the bound alone decides.
A program may use at most 64 MiB of HBM per device.

v0:
```python
import jax
import jax.numpy as jnp
from jax import lax
from jax.sharding import PartitionSpec as P


def matmul(first, second):
    return jnp.einsum("sij,sjk->sik", first, second, precision=lax.Precision.HIGHEST)


def per_device(transfer, hamiltonian, kept):
    col_count = transfer.shape[0]
    sectors = transfer.shape[1]
    width = transfer.shape[2]
    eye = jnp.broadcast_to(jnp.eye(width, dtype=jnp.float32), (sectors, width, width))
    group = transfer[0]
    column = 1
    group = matmul(group, transfer[column])
    groups = lax.all_gather(group[None], "col", axis=0, tiled=True)
    place = lax.axis_index("col")
    total = lax.axis_size("col")

    def select_left_side(step, acc):
        return matmul(acc, groups[step])

    prior_environment = lax.fori_loop(0, place, select_left_side, eye)

    def take_high(step, acc):
        return matmul(groups[total - 1 - step], acc)

    after = lax.fori_loop(0, total - 1 - place, take_high, eye)
    whole = matmul(matmul(prior_environment, group), after)
    lefts = [prior_environment]
    column = 1
    lefts.append(matmul(lefts[-1], transfer[column - 1]))
    right_environments = [after]
    column = 1
    right_environments.insert(0, matmul(transfer[column], right_environments[0]))
    column_positions = jnp.arange(width, dtype=jnp.int32)
    masked_list = []
    partial_results = []
    for column in range(col_count):
        mask = (column_positions[None, :] < kept[column][:, None]).astype(jnp.float32)
        masked = lefts[column] * mask[:, None, :]
        masked_list.append(masked)
        inner_contraction = jnp.einsum(
            "sji,sjk->sik", masked, whole, precision=lax.Precision.HIGHEST
        )
        inner_contraction = jnp.einsum(
            "sik,slk->sil",
            inner_contraction,
            right_environments[column],
            precision=lax.Precision.HIGHEST,
        )
        partial_results.append(
            jnp.einsum(
                "sil,tsil->t",
                inner_contraction,
                hamiltonian[column],
                precision=lax.Precision.HIGHEST,
            )
        )
    partial_value = jnp.stack(partial_results, axis=0)
    norm = jnp.sum(whole * whole)
    partial_value, norm = lax.psum((partial_value, norm), "sec")
    scale = float(width * sectors * lax.axis_size("sec"))
    energy = scale * partial_value / norm
    left_env = jnp.stack(masked_list, axis=0)
    return (left_env, energy)


def solution(mesh):
    in_specs = (P("col", "sec", None, None), P("col", None, "sec", None, None), P("col", "sec"))
    out_specs = (P("col", "sec", None, None), P("col", None))
    return jax.shard_map(
        per_device, mesh=mesh, in_specs=in_specs, out_specs=out_specs, check_vma=False
    )
```

profile of v0, /device:TPU:1, one launch (start us, length us, event | category | flops | bytes accessed | tf_op | source)
XLA Modules:
  0.0 192.9 jit_solution(6543052276919788004)
XLA Ops:
  7.2 2.1 %fusion.21 = f32[256,256]{1,0:T(8,128)} fusion(f32[2,1,256,256]{3,2,1,0:T(8,128)} %param.7), kind=kOutput, calls=%fused_computation.31 | convolution fusion | flops 201326592 | bytes 786432 | tf_op jit(solution)/shard_map/sij,sjk->sik/dot_general | solution.py:8
  9.5 1.4 fusion.34
  12.2 1.5 slice_bitcast_fusion.1
  13.8 98.3 %all-gather.3.cloned.1.call-done = f32[8192,256]{1,0:T(8,128)} async-done(((f32[256,256]{1,0:T(8,128)}), f32[8192,256]{1,0:T(8,128)}) %all-gather.3.cloned.1.call-update) | async-done | bytes 8388624 | tf_op jit(solution)/shard_map/all_gather | solution.py:19
  112.9 43.4 %while.23 = (s32[]{:T(128)}, f32[1,256,256]{2,1,0:T(8,128)S(1)}, s32[]{:T(128)}, f32[32,1,256,256]{3,2,1,0:T(8,128)}, s32[]{:T(128)}, /*index=5*/s32[]{:T(128)}, s32[]{:T(128)}, s32[]{:T(128)}) while((s32[]{:T(128)}, f32[1,256,256]{2,1,0:T(8,128)S(1)}, s32[]{:T(128)}, f32[32,1,256,256]{3,2,1,0:T(8,128)}, s32[]{:T(128)}, /*index=5*/s32[]{:T(128)}, ...), condition=%wide.region_3.0_spmd, body=%wide.region_2.0_spmd.sunk | while | flops 201326592 | bytes 1310855 | solution.py:31
  112.9 1.3 convolution_bitcast_fusion.9
  117.1 1.3 convolution_bitcast_fusion.9
  118.5 1.3 convolution_bitcast_fusion.9
  119.9 1.3 convolution_bitcast_fusion.9
  121.3 1.3 convolution_bitcast_fusion.9
  122.7 1.3 convolution_bitcast_fusion.9
  124.1 1.3 convolution_bitcast_fusion.9
  128.2 1.3 convolution_bitcast_fusion.9
  129.6 1.3 convolution_bitcast_fusion.9
  131.0 1.3 convolution_bitcast_fusion.9
  132.4 1.3 convolution_bitcast_fusion.9
  133.8 1.3 convolution_bitcast_fusion.9
  135.2 1.3 convolution_bitcast_fusion.9
  136.6 1.3 convolution_bitcast_fusion.9
  139.4 1.3 convolution_bitcast_fusion.9
  140.8 1.3 convolution_bitcast_fusion.9
  142.2 1.3 convolution_bitcast_fusion.9
  143.6 1.3 convolution_bitcast_fusion.9
  144.9 1.3 convolution_bitcast_fusion.9
  146.3 1.3 convolution_bitcast_fusion.9
  150.5 1.3 convolution_bitcast_fusion.9
  151.9 1.3 convolution_bitcast_fusion.9
  153.3 1.3 convolution_bitcast_fusion.9
  154.7 1.3 convolution_bitcast_fusion.9
  160.5 4.8 %convolution_bitcast_fusion.5 = f32[1,3]{1,0:T(1,128)S(1)} fusion(f32[3,256,256]{2,1,0:T(8,128)S(1)} %get-tuple-element.109, f32[256,256,1]{1,0,2:T(8,128)S(1)} %convolution_bitcast_fusion.3), kind=kOutput, calls=%fused_computation.14 | convolution fusion | flops 2359296 | bytes 1048588 | tf_op jit(solution)/shard_map/sil,tsil->t/dot_general | solution.py:56
  165.3 4.9 %convolution_bitcast_fusion.4 = f32[1,3]{1,0:T(1,128)S(1)} fusion(f32[3,256,256]{2,1,0:T(8,128)S(1)} %get-tuple-element.110, f32[256,256,1]{1,0,2:T(8,128)S(1)} %convolution_bitcast_fusion.2), kind=kOutput, calls=%fused_computation.13 | convolution fusion | flops 2359296 | bytes 1048588 | tf_op jit(solution)/shard_map/sil,tsil->t/dot_general | solution.py:56
  170.2 13.8 %all-reduce = (f32[2,3]{1,0:T(2,128)S(1)}, f32[]{:T(128)}) all-reduce(f32[2,3]{1,0:T(2,128)S(1)} %pad_maximum_fusion.1, f32[]{:T(128)} %get-tuple-element.113), channel_id=1, replica_groups=mesh['col'=32,'sec'=8] {'sec'}, use_global_device_ids=true, to_apply=%region_4.0 | all-reduce | flops 7 | bytes 56 | tf_op jit(solution)/shard_map/psum | solution.py:65
  (62 shorter events, 18.4 us)
Async XLA Ops:
  7.2 105.0 %all-gather.3.cloned.1.call-start = ((), (), s32[]{:S(2)}) async-start(), calls=%async_computation | async-start | bytes 8650752 | tf_op jit(solution)/shard_map/all_gather | solution.py:19
  9.3 102.8 %copy-start = (f32[256,256]{1,0:T(8,128)S(1)}, f32[256,256]{1,0:T(8,128)}, u32[]{:S(2)}) copy-start(f32[256,256]{1,0:T(8,128)} %fusion.21) | copy-start | bytes 786436
  12.2 144.0 %copy-start.1 = (f32[2,1,256,256]{3,2,1,0:T(8,128)S(1)}, f32[2,1,256,256]{3,2,1,0:T(8,128)}, u32[]{:S(2)}) copy-start(f32[2,1,256,256]{3,2,1,0:T(8,128)} %param.7) | copy-start | bytes 1572868
Sparse Core Ops, SparseCore 0:
  11.1 100.9 all-gather.2
where the time goes:
time: 196 us; the launch traced here: 193 us
  waiting for transfers between devices  98.4 us (50%)
  matrix products  57.9 us (30%)
  between operations  14.2 us (7%)
  blocking collectives  13.8 us (7%)
  local copies, waits for them, and re-layouts  3.77 us (2%)
  other arithmetic  3.41 us (2%)
    all_gather x1, waiting for transfers between devices, per_device(): groups = lax.all_gather(group[None], 'col', axis=0, tiled=True)  98.3 us
    dot_general x36, matrix products, matmul(): jnp.einsum('sij,sjk->sik', first, second, precision=lax.Precision.HIGHEST)  46.2 us
    psum x1, blocking collectives, per_device(): partial_value, norm = lax.psum((partial_value, norm), 'sec')  13.8 us
    dot_general x2, matrix products, per_device(): jnp.einsum('sil,tsil->t', inner_contraction, hamiltonian[column], precisi...  9.71 us
  transfers between devices with their start and end apart: 1, of which 1 were waited for; matrix products, arithmetic and copies ran while one was open for 2% of the time, Pallas kernels for 0%

commit v1 on v0

v1 whole, which is shorter than its diff:
```python
import jax
import jax.numpy as jnp
from jax import lax
from jax.experimental import pallas as pl
from jax.experimental.pallas import tpu as pltpu
from jax.sharding import PartitionSpec as P

MESH = pl.DeviceIdType.MESH
F32 = jnp.float32
BF16 = jnp.bfloat16
Y = 4
Z = 8
S = 8
N = 256
HALF = N // 2
QUARTER = N // 4
TERMS = 3
NN = (((1,), (0,)), ((), ()))
NT = (((1,), (1,)), ((), ()))
TN = (((0,), (0,)), ((), ()))


def split(x):
    high = x.astype(BF16)
    return high, (x - high.astype(F32)).astype(BF16)


def mm(a, b, dims=NN):
    ah, al = split(a)
    bh, bl = split(b)

    def dot(p, q):
        return lax.dot_general(p, q, dims, preferred_element_type=F32)

    return dot(ah, bh) + (dot(ah, bl) + dot(al, bh))


def kernel(
    t_hbm, h_hbm, kept_ref,
    left_hbm, energy_ref,
    t, h, g, r, acc_p, acc_m, post, lout, red,
    load_sem, store_sem, g_send, g_recv, z_send, z_recv, y_send, y_recv, s_send, s_recv,
):
    col = lax.axis_index("col")
    sec = lax.axis_index("sec")
    y = lax.rem(col, Y)
    z = col // Y

    def at_y(d):
        return z * Y + lax.rem(y + d + Y, Y)

    def at_z(d):
        return lax.rem(z + d + Z, Z) * Y + y

    loads = []
    for c in range(2):
        loads.append(pltpu.make_async_copy(t_hbm.at[c, 0], t.at[c], load_sem.at[c]))
    loads.append(pltpu.make_async_copy(h_hbm.at[:, :, 0], h, load_sem.at[2]))
    for copy in loads:
        copy.start()

    barrier = pltpu.get_barrier_semaphore()
    partners = [(at_y(1), sec), (at_y(-1), sec), (at_z(1), sec), (at_z(-1), sec)]
    partners += [(col, lax.rem(sec + d, S)) for d in range(1, S)]
    for partner in partners:
        pl.semaphore_signal(barrier, inc=1, device_id=partner, device_id_type=MESH)

    sends = []

    def send(ref, target, send_sem, recv_sem):
        copy = pltpu.make_async_remote_copy(
            src_ref=ref, dst_ref=ref, send_sem=send_sem, recv_sem=recv_sem,
            device_id=target, device_id_type=MESH,
        )
        copy.start()
        sends.append(copy)

    def arrived(ref, send_sem, recv_sem):
        pltpu.make_async_remote_copy(
            src_ref=ref, dst_ref=ref, send_sem=send_sem, recv_sem=recv_sem,
            device_id=(col, sec), device_id_type=MESH,
        ).wait_recv()

    top = pl.ds(0, HALF)
    bottom = pl.ds(HALF, HALF)
    loads[0].wait()
    loads[1].wait()
    g[y] = mm(t[0], t[1])
    pl.semaphore_wait(barrier, len(partners))

    y_plus, y_minus = (at_y(1), sec), (at_y(-1), sec)
    z_plus, z_minus = (at_z(1), sec), (at_z(-1), sec)
    before, after, opposite = lax.rem(y + 3, Y), lax.rem(y + 1, Y), lax.rem(y + 2, Y)

    def g_copy(direction, index, block, rows):
        target = y_plus if direction == 0 else y_minus
        send(g.at[block, rows], target, g_send.at[direction, index], g_recv.at[direction, index])

    def g_wait(direction, index, block, rows):
        arrived(g.at[block, rows], g_send.at[direction, index], g_recv.at[direction, index])

    g_copy(0, 0, y, top)
    g_copy(1, 0, y, bottom)
    g_copy(0, 1, y, bottom)
    g_copy(1, 1, y, top)
    g_wait(0, 0, before, top)
    g_copy(0, 2, before, top)
    g_wait(1, 0, after, bottom)
    g_copy(1, 2, after, bottom)
    g_wait(0, 1, before, bottom)
    g_wait(1, 1, after, top)
    g_wait(0, 2, opposite, top)
    g_wait(1, 2, opposite, bottom)

    low = mm(g[0], g[1])
    high = mm(g[2], g[3])
    r[z] = mm(low, high)

    def quarter(q):
        return pl.ds(pl.multiple_of(lax.rem(y + q, Y) * QUARTER, QUARTER), QUARTER)

    def z_block(direction, step):
        return lax.rem(z - step + Z, Z) if direction == 0 else lax.rem(z + step, Z)

    def z_copy(direction, step, part):
        ref = r.at[z_block(direction, step - 1), quarter(2 * direction + part)]
        target = z_plus if direction == 0 else z_minus
        send(ref, target, z_send.at[direction, step - 1, part], z_recv.at[direction, step - 1, part])

    def z_wait(direction, step, part):
        ref = r.at[z_block(direction, step), quarter(2 * direction + part)]
        arrived(ref, z_send.at[direction, step - 1, part], z_recv.at[direction, step - 1, part])

    def y_copy(direction, step, part):
        ref = r.at[z_block(direction, step), quarter(2 * direction + part)]
        target = y_plus if part == 0 else y_minus
        send(ref, target, y_send.at[direction, step - 1, part], y_recv.at[direction, step - 1, part])

    def y_wait(direction, step, part):
        ref = r.at[z_block(direction, step), quarter(2 * direction + (3 if part == 0 else 2))]
        arrived(ref, y_send.at[direction, step - 1, part], y_recv.at[direction, step - 1, part])

    for part in range(2):
        for direction in range(2):
            z_copy(direction, 1, part)

    acc_p[...] = low
    acc_m[...] = high

    @pl.when(y == 0)
    def _():
        acc_m[...] = mm(g[1], acc_m[...])

    @pl.when(y == 1)
    def _():
        acc_p[...] = g[0]

    @pl.when(y == 2)
    def _():
        acc_m[...] = g[3]

    @pl.when(y == 3)
    def _():
        acc_p[...] = mm(acc_p[...], g[2])

    row = lax.broadcasted_iota(jnp.int32, (N, N), 0)
    column = lax.broadcasted_iota(jnp.int32, (N, N), 1)

    @pl.when(y == 0)
    def _():
        acc_p[...] = (row == column).astype(F32)

    @pl.when(y == 3)
    def _():
        acc_m[...] = (row == column).astype(F32)

    def take_blocks(step):
        for direction in range(2):
            for part in range(2):
                y_wait(direction, step, part)
        plus = z_block(0, step)
        minus = z_block(1, step)

        @pl.when(step <= z)
        def _():
            acc_p[...] = mm(r[plus], acc_p[...])

        @pl.when(step == z + 1)
        def _():
            post[...] = r[plus]

        @pl.when(step > z + 1)
        def _():
            post[...] = mm(r[plus], post[...])

        @pl.when(step <= Z - 1 - z)
        def _():
            acc_m[...] = mm(acc_m[...], r[minus])

        @pl.when(step == Z - z)
        def _():
            post[...] = r[minus]

        @pl.when(step > Z - z)
        def _():
            post[...] = mm(post[...], r[minus])

    for step in range(1, 5):
        for part in range(2):
            for direction in range(2):
                z_wait(direction, step, part)
                if step < 4:
                    z_copy(direction, step + 1, part)
                    y_copy(direction, step, part)
        if step > 1:
            take_blocks(step - 1)

    middle = lax.rem(z + 4, Z)

    @pl.when(z < 4)
    def _():
        acc_m[...] = mm(acc_m[...], r[middle])

    @pl.when(z < 3)
    def _():
        acc_m[...] = mm(acc_m[...], post[...])

    @pl.when(z >= 4)
    def _():
        acc_p[...] = mm(r[middle], acc_p[...])

    @pl.when(z > 4)
    def _():
        acc_p[...] = mm(post[...], acc_p[...])

    left0 = acc_p[...]
    right1 = acc_m[...]
    left1 = mm(left0, t[0])
    right0 = mm(t[1], right1)
    lout[0] = jnp.where(column < kept_ref[0, 0], left0, 0.0)
    lout[1] = jnp.where(column < kept_ref[0, 1], left1, 0.0)
    stores = []
    for c in range(2):
        copy = pltpu.make_async_copy(lout.at[c], left_hbm.at[c, 0], store_sem.at[c])
        copy.start()
        stores.append(copy)
    whole = mm(left1, right0)
    loads[2].wait()

    def fold(x):
        return jnp.sum(x, axis=0, keepdims=True)

    def lanes(x):
        x = fold(x)
        return x[:, :128] + x[:, 128:]

    rows = []
    for c, (left, right) in enumerate(((left0, right0), (left1, right1))):
        inner = mm(mm(left, whole, TN), right, NT)
        inner = jnp.where(row < kept_ref[0, c], inner, 0.0)
        for k in range(TERMS):
            rows.append(lanes(inner * h[c, k]))
    rows.append(lanes(whole * whole))
    rows.append(jnp.zeros((1, 128), F32))
    red[sec] = jnp.concatenate(rows, axis=0)

    for d in range(1, S):
        send(red.at[sec], (col, lax.rem(sec + d, S)), s_send.at[d], s_recv.at[d])
    for d in range(1, S):
        arrived(red.at[lax.rem(sec - d + S, S)], s_send.at[d], s_recv.at[d])
    total = red[0]
    for k in range(1, S):
        total = total + red[k]
    total = jnp.sum(total, axis=1, keepdims=True)
    values = (float(N * S) * total[0:6]) / total[6:7]
    place = 3 * lax.broadcasted_iota(jnp.int32, (2, 3), 0) + lax.broadcasted_iota(jnp.int32, (2, 3), 1)
    energy = jnp.zeros((2, 3), F32)
    for k in range(6):
        energy = jnp.where(place == k, values[k:k + 1], energy)
    energy_ref[...] = energy

    for copy in sends:
        copy.wait_send()
    for copy in stores:
        copy.wait()


def per_device(transfer, hamiltonian, kept):
    dma = pltpu.SemaphoreType.DMA
    return pl.pallas_call(
        kernel,
        name="chain",
        out_shape=(
            jax.ShapeDtypeStruct((2, 1, N, N), F32),
            jax.ShapeDtypeStruct((2, TERMS), F32),
        ),
        in_specs=[
            pl.BlockSpec(memory_space=pl.ANY),
            pl.BlockSpec(memory_space=pl.ANY),
            pl.BlockSpec(memory_space=pltpu.SMEM),
        ],
        out_specs=(
            pl.BlockSpec(memory_space=pl.ANY),
            pl.BlockSpec(memory_space=pltpu.VMEM),
        ),
        scratch_shapes=[
            pltpu.VMEM((2, N, N), F32),
            pltpu.VMEM((2, TERMS, N, N), F32),
            pltpu.VMEM((Y, N, N), F32),
            pltpu.VMEM((Z, N, N), F32),
            pltpu.VMEM((N, N), F32),
            pltpu.VMEM((N, N), F32),
            pltpu.VMEM((N, N), F32),
            pltpu.VMEM((2, N, N), F32),
            pltpu.VMEM((S, 8, 128), F32),
            dma((3,)),
            dma((2,)),
            dma((2, 3)),
            dma((2, 3)),
            dma((2, 4, 2)),
            dma((2, 4, 2)),
            dma((2, 3, 2)),
            dma((2, 3, 2)),
            dma((S,)),
            dma((S,)),
        ],
        compiler_params=pltpu.CompilerParams(collective_id=0, has_side_effects=True),
    )(transfer, hamiltonian, kept.T)


def solution(mesh):
    in_specs = (P("col", "sec", None, None), P("col", None, "sec", None, None), P("col", "sec"))
    out_specs = (P("col", "sec", None, None), P("col", None))
    return jax.shard_map(
        per_device, mesh=mesh, in_specs=in_specs, out_specs=out_specs, check_vma=False
    )
```

time: 196 us -> 49.3 us (0.25); the launches traced: 193 us -> 49.1 us
  waiting for transfers between devices: 98.4 us -> 0 us
  matrix products: 57.9 us -> 0 us
  Pallas kernels: 0 us -> 45.4 us
  blocking collectives: 13.8 us -> 0 us
  between operations: 14.2 us -> 0.64 us
  other arithmetic: 3.41 us -> 0 us
    all_gather x1 -> x0, waiting for transfers between devices: 98.3 us -> none  [per_device(): groups = lax.all_gather(group[None], 'col', axis=0, tiled=True)]
    dot_general x42 -> x0, matrix products: 57.9 us -> none  [the longest x36 46.2 us: matmul(): jnp.einsum('sij,sjk->sik', first, second, precision=lax.Precision.HIGHEST)]
    pallas_call x0 -> x1, Pallas kernels: none -> 45.4 us  [per_device(): pl.pallas_call(kernel, name='chain', out_shape=(jax.ShapeDtypeStruct((2,...]
    psum x1 -> x0, blocking collectives: 13.8 us -> none  [per_device(): partial_value, norm = lax.psum((partial_value, norm), 'sec')]
    unnamed x4 -> x2, local copies, waits for them, and re-layouts: 0.01 us -> 3.07 us
  transfers between devices with their start and end apart: 1 -> 0, of which waited for: 1 -> 0; matrix products, arithmetic and copies ran while one was open for 2% -> 0% of each run, Pallas kernels for 0% -> 0%
where the time goes in v1:
time: 49.3 us; the launch traced here: 49.1 us
  Pallas kernels  45.4 us (92%)
  local copies, waits for them, and re-layouts  3.07 us (6%)
  between operations  0.64 us (1%)
    pallas_call x1, Pallas kernels, per_device(): pl.pallas_call(kernel, name='chain', out_shape=(jax.ShapeDtypeStruct((2,...  45.4 us
    unnamed x2, local copies, waits for them, and re-layouts  3.07 us

profile of v1, /device:TPU:1, one launch (start us, length us, event | category | flops | bytes accessed | tf_op | source)
XLA Modules:
  0.0 49.1 jit_solution(1357925901079898617)
XLA Ops:
  0.6 45.4 %chain.1 = (f32[2,1,256,256]{3,2,1,0:T(8,128)}, f32[2,3]{1,0:T(2,128)}) custom-call(f32[2,1,256,256]{3,2,1,0:T(8,128)} %t_hbm.1, f32[2,3,1,256,256]{4,3,2,1,0:T(8,128)} %h_hbm.1, s32[1,2]{1,0:T(1,128)} %bitcast.1), custom_call_target="tpu_custom_call" | custom-call | tf_op jit(solution)/shard_map/chain/pallas_call | solution.py:290
  46.0 1.9 %copy.7 = f32[2,1,256,256]{3,2,1,0:T(8,128)} copy(f32[2,1,256,256]{3,2,1,0:T(8,128)} %get-tuple-element.4) | data formatting | bytes 1048576
  47.9 1.2 %copy.8 = f32[2,3]{1,0:T(2,128)} copy(f32[2,3]{1,0:T(2,128)} %get-tuple-element.5) | data formatting | bytes 48

commit v2 on v1

--- a/solution.py
+++ b/solution.py
@@ -14,6 +14,8 @@
 N = 256
 HALF = N // 2
 QUARTER = N // 4
+PARTS = 4
+ROWS = HALF // PARTS
 TERMS = 3
 NN = (((1,), (0,)), ((), ()))
 NT = (((1,), (1,)), ((), ()))
@@ -37,9 +39,9 @@
 
 def kernel(
     t_hbm, h_hbm, kept_ref,
-    left_hbm, energy_ref,
-    t, h, g, r, acc_p, acc_m, post, lout, red,
-    load_sem, store_sem, g_send, g_recv, z_send, z_recv, y_send, y_recv, s_send, s_recv,
+    lout, sums_ref,
+    t, h, g, r, acc_p, acc_m, post, left1_ref, right0_ref, ahead, whole_ref, red,
+    load_sem, g_send, g_recv, z_send, z_recv, y_send, y_recv, s_send, s_recv,
 ):
     col = lax.axis_index("col")
     sec = lax.axis_index("sec")
@@ -85,7 +87,7 @@
     bottom = pl.ds(HALF, HALF)
     loads[0].wait()
     loads[1].wait()
-    g[y] = mm(t[0], t[1])
+    g[y, top] = mm(t[0, top], t[1])
     pl.semaphore_wait(barrier, len(partners))
 
     y_plus, y_minus = (at_y(1), sec), (at_y(-1), sec)
@@ -100,6 +102,7 @@
         arrived(g.at[block, rows], g_send.at[direction, index], g_recv.at[direction, index])
 
     g_copy(0, 0, y, top)
+    g[y, bottom] = mm(t[0, bottom], t[1])
     g_copy(1, 0, y, bottom)
     g_copy(0, 1, y, bottom)
     g_copy(1, 1, y, top)
@@ -116,31 +119,33 @@
     high = mm(g[2], g[3])
     r[z] = mm(low, high)
 
-    def quarter(q):
-        return pl.ds(pl.multiple_of(lax.rem(y + q, Y) * QUARTER, QUARTER), QUARTER)
+    def chunk(direction, part, shift=0):
+        start = lax.rem(y * QUARTER + direction * HALF + part * ROWS + shift, N)
+        return pl.ds(pl.multiple_of(start, ROWS), ROWS)
 
     def z_block(direction, step):
         return lax.rem(z - step + Z, Z) if direction == 0 else lax.rem(z + step, Z)
 
     def z_copy(direction, step, part):
-        ref = r.at[z_block(direction, step - 1), quarter(2 * direction + part)]
+        ref = r.at[z_block(direction, step - 1), chunk(direction, part)]
         target = z_plus if direction == 0 else z_minus
         send(ref, target, z_send.at[direction, step - 1, part], z_recv.at[direction, step - 1, part])
 
     def z_wait(direction, step, part):
-        ref = r.at[z_block(direction, step), quarter(2 * direction + part)]
+        ref = r.at[z_block(direction, step), chunk(direction, part)]
         arrived(ref, z_send.at[direction, step - 1, part], z_recv.at[direction, step - 1, part])
 
     def y_copy(direction, step, part):
-        ref = r.at[z_block(direction, step), quarter(2 * direction + part)]
-        target = y_plus if part == 0 else y_minus
+        ref = r.at[z_block(direction, step), chunk(direction, part)]
+        target = y_plus if part < PARTS // 2 else y_minus
         send(ref, target, y_send.at[direction, step - 1, part], y_recv.at[direction, step - 1, part])
 
     def y_wait(direction, step, part):
-        ref = r.at[z_block(direction, step), quarter(2 * direction + (3 if part == 0 else 2))]
+        shift = 3 * QUARTER if part < PARTS // 2 else QUARTER
+        ref = r.at[z_block(direction, step), chunk(direction, part, shift)]
         arrived(ref, y_send.at[direction, step - 1, part], y_recv.at[direction, step - 1, part])
 
-    for part in range(2):
+    for part in range(PARTS):
         for direction in range(2):
             z_copy(direction, 1, part)
 
@@ -174,9 +179,15 @@
     def _():
         acc_m[...] = (row == column).astype(F32)
 
+    def lefts_from(left0):
+        left1 = mm(left0, t[0])
+        left1_ref[...] = left1
+        lout[0] = jnp.where(column < kept_ref[0, 0], left0, 0.0)
+        lout[1] = jnp.where(column < kept_ref[0, 1], left1, 0.0)
+
     def take_blocks(step):
         for direction in range(2):
-            for part in range(2):
+            for part in range(PARTS):
                 y_wait(direction, step, part)
         plus = z_block(0, step)
         minus = z_block(1, step)
@@ -205,16 +216,29 @@
         def _():
             post[...] = mm(post[...], r[minus])
 
-    for step in range(1, 5):
-        for part in range(2):
+    for step in range(1, 4):
+        for part in range(PARTS):
             for direction in range(2):
                 z_wait(direction, step, part)
-                if step < 4:
-                    z_copy(direction, step + 1, part)
-                    y_copy(direction, step, part)
+                z_copy(direction, step + 1, part)
+                y_copy(direction, step, part)
         if step > 1:
             take_blocks(step - 1)
-
+    take_blocks(3)
+
+    @pl.when(z < 4)
+    def _():
+        lefts_from(acc_p[...])
+        ahead[...] = mm(left1_ref[...], t[1])
+
+    @pl.when(z >= 4)
+    def _():
+        right0_ref[...] = mm(t[1], acc_m[...])
+        ahead[...] = mm(t[0], right0_ref[...])
+
+    for part in range(PARTS):
+        for direction in range(2):
+            z_wait(direction, 4, part)
     middle = lax.rem(z + 4, Z)
 
     @pl.when(z < 4)
@@ -233,18 +257,18 @@
     def _():
         acc_p[...] = mm(post[...], acc_p[...])
 
-    left0 = acc_p[...]
-    right1 = acc_m[...]
-    left1 = mm(left0, t[0])
-    right0 = mm(t[1], right1)
-    lout[0] = jnp.where(column < kept_ref[0, 0], left0, 0.0)
-    lout[1] = jnp.where(column < kept_ref[0, 1], left1, 0.0)
-    stores = []
-    for c in range(2):
-        copy = pltpu.make_async_copy(lout.at[c], left_hbm.at[c, 0], store_sem.at[c])
-        copy.start()
-        stores.append(copy)
-    whole = mm(left1, right0)
+    @pl.when(z < 4)
+    def _():
+        whole_ref[...] = mm(ahead[...], acc_m[...])
+        right0_ref[...] = mm(t[1], acc_m[...])
+
+    @pl.when(z >= 4)
+    def _():
+        whole_ref[...] = mm(acc_p[...], ahead[...])
+        lefts_from(acc_p[...])
+
+    left0, left1, right0, right1 = acc_p[...], left1_ref[...], right0_ref[...], acc_m[...]
+    whole = whole_ref[...]
     loads[2].wait()
 
     def fold(x):
@@ -264,13 +288,26 @@
     rows.append(jnp.zeros((1, 128), F32))
     red[sec] = jnp.concatenate(rows, axis=0)
 
-    for d in range(1, S):
+    for d in (4, 3, 5, 2, 6, 1, 7):
         send(red.at[sec], (col, lax.rem(sec + d, S)), s_send.at[d], s_recv.at[d])
     for d in range(1, S):
         arrived(red.at[lax.rem(sec - d + S, S)], s_send.at[d], s_recv.at[d])
     total = red[0]
     for k in range(1, S):
         total = total + red[k]
+    sums_ref[...] = total
+
+    for copy in sends:
+        copy.wait_send()
+
+
+def finish(lefts, sums_ref, left_hbm, energy_ref, sems):
+    stores = []
+    for c in range(2):
+        copy = pltpu.make_async_copy(lefts.at[c], left_hbm.at[c, 0], sems.at[c])
+        copy.start()
+        stores.append(copy)
+    total = sums_ref[...]
     total = jnp.sum(total, axis=1, keepdims=True)
     values = (float(N * S) * total[0:6]) / total[6:7]
     place = 3 * lax.broadcasted_iota(jnp.int32, (2, 3), 0) + lax.broadcasted_iota(jnp.int32, (2, 3), 1)
@@ -278,54 +315,53 @@
     for k in range(6):
         energy = jnp.where(place == k, values[k:k + 1], energy)
     energy_ref[...] = energy
-
-    for copy in sends:
-        copy.wait_send()
     for copy in stores:
         copy.wait()
 
 
 def per_device(transfer, hamiltonian, kept):
     dma = pltpu.SemaphoreType.DMA
-    return pl.pallas_call(
+    vmem = pl.BlockSpec(memory_space=pltpu.VMEM)
+    lefts, sums = pl.pallas_call(
         kernel,
         name="chain",
-        out_shape=(
-            jax.ShapeDtypeStruct((2, 1, N, N), F32),
-            jax.ShapeDtypeStruct((2, TERMS), F32),
-        ),
+        out_shape=(pltpu.VMEM((2, N, N), F32), pltpu.VMEM((8, 128), F32)),
         in_specs=[
             pl.BlockSpec(memory_space=pl.ANY),
             pl.BlockSpec(memory_space=pl.ANY),
             pl.BlockSpec(memory_space=pltpu.SMEM),
         ],
-        out_specs=(
-            pl.BlockSpec(memory_space=pl.ANY),
-            pl.BlockSpec(memory_space=pltpu.VMEM),
-        ),
+        out_specs=(vmem, vmem),
         scratch_shapes=[
             pltpu.VMEM((2, N, N), F32),
             pltpu.VMEM((2, TERMS, N, N), F32),
             pltpu.VMEM((Y, N, N), F32),
             pltpu.VMEM((Z, N, N), F32),
-            pltpu.VMEM((N, N), F32),
-            pltpu.VMEM((N, N), F32),
-            pltpu.VMEM((N, N), F32),
-            pltpu.VMEM((2, N, N), F32),
+            *[pltpu.VMEM((N, N), F32)] * 7,
             pltpu.VMEM((S, 8, 128), F32),
             dma((3,)),
-            dma((2,)),
             dma((2, 3)),
             dma((2, 3)),
-            dma((2, 4, 2)),
-            dma((2, 4, 2)),
-            dma((2, 3, 2)),
-            dma((2, 3, 2)),
+            dma((2, 4, PARTS)),
+            dma((2, 4, PARTS)),
+            dma((2, 3, PARTS)),
+            dma((2, 3, PARTS)),
             dma((S,)),
             dma((S,)),
         ],
         compiler_params=pltpu.CompilerParams(collective_id=0, has_side_effects=True),
     )(transfer, hamiltonian, kept.T)
+    return pl.pallas_call(
+        finish,
+        name="finish",
+        out_shape=(
+            jax.ShapeDtypeStruct((2, 1, N, N), F32),
+            jax.ShapeDtypeStruct((2, TERMS), F32),
+        ),
+        in_specs=[vmem, vmem],
+        out_specs=(pl.BlockSpec(memory_space=pl.ANY), vmem),
+        scratch_shapes=[dma((2,))],
+    )(*(pltpu.with_memory_space_constraint(x, pltpu.VMEM) for x in (lefts, sums)))
 
 
 def solution(mesh):

time: 49.3 us -> 47.3 us (0.959)
  local copies, waits for them, and re-layouts: 3.07 us -> 0 us
  Pallas kernels: 45.4 us -> 46.5 us
    unnamed x2 -> x0, local copies, waits for them, and re-layouts: 3.07 us -> none
    pallas_call x1 -> x2, Pallas kernels: 45.4 us -> 46.5 us  [the longest x1 45.1 us: per_device(): pl.pallas_call(kernel, name='chain', out_shape=(pltpu.VMEM((2, N, N), F32...]
where the time goes in v2:
time: 47.3 us; the launch traced here: 47.1 us
  Pallas kernels  46.5 us (98%)
  between operations  0.64 us (1%)
    pallas_call x1, Pallas kernels, per_device(): pl.pallas_call(kernel, name='chain', out_shape=(pltpu.VMEM((2, N, N), F32...  45.1 us
    pallas_call x1, Pallas kernels, per_device(): pl.pallas_call(finish, name='finish', out_shape=(jax.ShapeDtypeStruct((2,...  1.37 us

profile of v2, /device:TPU:1, one launch (start us, length us, event | category | flops | bytes accessed | tf_op | source)
XLA Modules:
  0.0 47.1 jit_solution(657576577962126422)
XLA Ops:
  0.6 45.1 %chain.1 = (f32[2,256,256]{2,1,0:T(8,128)S(1)}, f32[8,128]{1,0:T(8,128)S(1)}) custom-call(f32[2,1,256,256]{3,2,1,0:T(8,128)} %t_hbm.1, f32[2,3,1,256,256]{4,3,2,1,0:T(8,128)} %h_hbm.1, s32[1,2]{1,0:T(1,128)} %bitcast.1), custom_call_target="tpu_custom_call" | custom-call | tf_op jit(solution)/shard_map/chain/pallas_call | solution.py:325
  45.8 1.4 %finish.1 = (f32[2,1,256,256]{3,2,1,0:T(8,128)}, f32[2,3]{1,0:T(2,128)}) custom-call(f32[2,256,256]{2,1,0:T(8,128)S(1)} %get-tuple-element.4.lefts, f32[8,128]{1,0:T(8,128)S(1)} %get-tuple-element.5.sums_ref), custom_call_target="tpu_custom_call" | custom-call | tf_op jit(solution)/shard_map/finish/pallas_call | solution.py:354

commit v3 on v2

--- a/solution.py
+++ b/solution.py
@@ -40,7 +40,7 @@
 def kernel(
     t_hbm, h_hbm, kept_ref,
     lout, sums_ref,
-    t, h, g, r, acc_p, acc_m, post, left1_ref, right0_ref, ahead, whole_ref, red,
+    t, h, g, r, acc_p, acc_m, post, left1_ref, inner, red,
     load_sem, g_send, g_recv, z_send, z_recv, y_send, y_recv, s_send, s_recv,
 ):
     col = lax.axis_index("col")
@@ -58,8 +58,8 @@
     for c in range(2):
         loads.append(pltpu.make_async_copy(t_hbm.at[c, 0], t.at[c], load_sem.at[c]))
     loads.append(pltpu.make_async_copy(h_hbm.at[:, :, 0], h, load_sem.at[2]))
-    for copy in loads:
-        copy.start()
+    loads[0].start()
+    loads[1].start()
 
     barrier = pltpu.get_barrier_semaphore()
     partners = [(at_y(1), sec), (at_y(-1), sec), (at_z(1), sec), (at_z(-1), sec)]
@@ -87,6 +87,7 @@
     bottom = pl.ds(HALF, HALF)
     loads[0].wait()
     loads[1].wait()
+    loads[2].start()
     g[y, top] = mm(t[0, top], t[1])
     pl.semaphore_wait(barrier, len(partners))
 
@@ -94,26 +95,53 @@
     z_plus, z_minus = (at_z(1), sec), (at_z(-1), sec)
     before, after, opposite = lax.rem(y + 3, Y), lax.rem(y + 1, Y), lax.rem(y + 2, Y)
 
-    def g_copy(direction, index, block, rows):
+    def g_rows(direction, index):
+        part = (index + 2 * direction) % 4
+        return pl.ds(part * QUARTER, QUARTER)
+
+    def g_copy(direction, index, block):
         target = y_plus if direction == 0 else y_minus
+        rows = g_rows(direction, index % 4)
         send(g.at[block, rows], target, g_send.at[direction, index], g_recv.at[direction, index])
 
-    def g_wait(direction, index, block, rows):
+    def g_wait(direction, index, block):
+        rows = g_rows(direction, index % 4)
         arrived(g.at[block, rows], g_send.at[direction, index], g_recv.at[direction, index])
 
-    g_copy(0, 0, y, top)
+    g_copy(0, 0, y)
+    g_copy(0, 1, y)
     g[y, bottom] = mm(t[0, bottom], t[1])
-    g_copy(1, 0, y, bottom)
-    g_copy(0, 1, y, bottom)
-    g_copy(1, 1, y, top)
-    g_wait(0, 0, before, top)
-    g_copy(0, 2, before, top)
-    g_wait(1, 0, after, bottom)
-    g_copy(1, 2, after, bottom)
-    g_wait(0, 1, before, bottom)
-    g_wait(1, 1, after, top)
-    g_wait(0, 2, opposite, top)
-    g_wait(1, 2, opposite, bottom)
+    for direction, index in ((1, 0), (1, 1), (0, 2), (1, 2), (0, 3), (1, 3)):
+        g_copy(direction, index, y)
+
+    loads[2].wait()
+    row = lax.broadcasted_iota(jnp.int32, (N, N), 0)
+    column = lax.broadcasted_iota(jnp.int32, (N, N), 1)
+    for c in range(2):
+        kept = row < kept_ref[0, c]
+        for k in range(TERMS):
+            h[c, k] = jnp.where(kept, h[c, k], 0.0)
+    for k in range(TERMS):
+
+        @pl.when(z < 4)
+        def _():
+            h[0, k] = mm(h[0, k], t[1])
+
+        @pl.when(z >= 4)
+        def _():
+            h[1, k] = mm(t[0], h[1, k])
+
+    neighbours = (before, after)
+    for index in range(2):
+        for direction in range(2):
+            g_wait(direction, index, neighbours[direction])
+            g_copy(direction, index + 4, neighbours[direction])
+    for index in range(2, 4):
+        for direction in range(2):
+            g_wait(direction, index, neighbours[direction])
+    for index in range(4, 6):
+        for direction in range(2):
+            g_wait(direction, index, opposite)
 
     low = mm(g[0], g[1])
     high = mm(g[2], g[3])
@@ -167,9 +195,6 @@
     @pl.when(y == 3)
     def _():
         acc_p[...] = mm(acc_p[...], g[2])
-
-    row = lax.broadcasted_iota(jnp.int32, (N, N), 0)
-    column = lax.broadcasted_iota(jnp.int32, (N, N), 1)
 
     @pl.when(y == 0)
     def _():
@@ -229,12 +254,19 @@
     @pl.when(z < 4)
     def _():
         lefts_from(acc_p[...])
-        ahead[...] = mm(left1_ref[...], t[1])
+        whole = mm(left1_ref[...], t[1])
+        inner[0] = mm(acc_p[...], whole, TN)
+        inner[1] = mm(left1_ref[...], whole, TN)
+        inner[2] = mm(whole, whole, TN)
 
     @pl.when(z >= 4)
     def _():
-        right0_ref[...] = mm(t[1], acc_m[...])
-        ahead[...] = mm(t[0], right0_ref[...])
+        right1 = acc_m[...]
+        right0 = mm(t[1], right1)
+        whole = mm(t[0], right0)
+        inner[0] = mm(whole, right0, NT)
+        inner[1] = mm(whole, right1, NT)
+        inner[2] = mm(whole, whole, NT)
 
     for part in range(PARTS):
         for direction in range(2):
@@ -257,39 +289,33 @@
     def _():
         acc_p[...] = mm(post[...], acc_p[...])
 
+    def lanes(x):
+        x = jnp.sum(x, axis=0, keepdims=True)
+        return x[:, :128] + x[:, 128:]
+
+    def reduce(inner0, inner1, gram):
+        rows = [lanes(inner0 * h[0, k]) for k in range(TERMS)]
+        rows += [lanes(inner1 * h[1, k]) for k in range(TERMS)]
+        rows += [lanes(inner[2] * gram), jnp.zeros((1, 128), F32)]
+        red[sec] = jnp.concatenate(rows, axis=0)
+
     @pl.when(z < 4)
     def _():
-        whole_ref[...] = mm(ahead[...], acc_m[...])
-        right0_ref[...] = mm(t[1], acc_m[...])
+        gram = mm(acc_m[...], acc_m[...], NT)
+        reduce(mm(inner[0], gram), mm(inner[1], gram), gram)
 
     @pl.when(z >= 4)
     def _():
-        whole_ref[...] = mm(acc_p[...], ahead[...])
-        lefts_from(acc_p[...])
-
-    left0, left1, right0, right1 = acc_p[...], left1_ref[...], right0_ref[...], acc_m[...]
-    whole = whole_ref[...]
-    loads[2].wait()
-
-    def fold(x):
-        return jnp.sum(x, axis=0, keepdims=True)
-
-    def lanes(x):
-        x = fold(x)
-        return x[:, :128] + x[:, 128:]
-
-    rows = []
-    for c, (left, right) in enumerate(((left0, right0), (left1, right1))):
-        inner = mm(mm(left, whole, TN), right, NT)
-        inner = jnp.where(row < kept_ref[0, c], inner, 0.0)
-        for k in range(TERMS):
-            rows.append(lanes(inner * h[c, k]))
-    rows.append(lanes(whole * whole))
-    rows.append(jnp.zeros((1, 128), F32))
-    red[sec] = jnp.concatenate(rows, axis=0)
+        gram = mm(acc_p[...], acc_p[...], TN)
+        reduce(mm(gram, inner[0]), mm(gram, inner[1]), gram)
 
     for d in (4, 3, 5, 2, 6, 1, 7):
         send(red.at[sec], (col, lax.rem(sec + d, S)), s_send.at[d], s_recv.at[d])
+
+    @pl.when(z >= 4)
+    def _():
+        lefts_from(acc_p[...])
+
     for d in range(1, S):
         arrived(red.at[lax.rem(sec - d + S, S)], s_send.at[d], s_recv.at[d])
     total = red[0]
@@ -304,9 +330,11 @@
 def finish(lefts, sums_ref, left_hbm, energy_ref, sems):
     stores = []
     for c in range(2):
-        copy = pltpu.make_async_copy(lefts.at[c], left_hbm.at[c, 0], sems.at[c])
-        copy.start()
-        stores.append(copy)
+        for k in range(4):
+            rows = pl.ds(k * QUARTER, QUARTER)
+            copy = pltpu.make_async_copy(lefts.at[c, rows], left_hbm.at[c, 0, rows], sems.at[c, k])
+            copy.start()
+            stores.append(copy)
     total = sums_ref[...]
     total = jnp.sum(total, axis=1, keepdims=True)
     values = (float(N * S) * total[0:6]) / total[6:7]
@@ -337,11 +365,12 @@
             pltpu.VMEM((2, TERMS, N, N), F32),
             pltpu.VMEM((Y, N, N), F32),
             pltpu.VMEM((Z, N, N), F32),
-            *[pltpu.VMEM((N, N), F32)] * 7,
+            *[pltpu.VMEM((N, N), F32)] * 4,
+            pltpu.VMEM((3, N, N), F32),
             pltpu.VMEM((S, 8, 128), F32),
             dma((3,)),
-            dma((2, 3)),
-            dma((2, 3)),
+            dma((2, 6)),
+            dma((2, 6)),
             dma((2, 4, PARTS)),
             dma((2, 4, PARTS)),
             dma((2, 3, PARTS)),
@@ -360,7 +389,7 @@
         ),
         in_specs=[vmem, vmem],
         out_specs=(pl.BlockSpec(memory_space=pl.ANY), vmem),
-        scratch_shapes=[dma((2,))],
+        scratch_shapes=[dma((2, 4))],
     )(*(pltpu.with_memory_space_constraint(x, pltpu.VMEM) for x in (lefts, sums)))
 
 

time: 47.3 us -> 47.5 us (level)
  no operation moved by 1% of the time
where the time goes in v3:
time: 47.5 us; the launch traced here: 47.4 us
  Pallas kernels  46.7 us (98%)
  between operations  0.64 us (1%)
    pallas_call x1, Pallas kernels, per_device(): pl.pallas_call(kernel, name='chain', out_shape=(pltpu.VMEM((2, N, N), F32...  45.3 us
    pallas_call x1, Pallas kernels, per_device(): pl.pallas_call(finish, name='finish', out_shape=(jax.ShapeDtypeStruct((2,...  1.41 us

profile of v3, /device:TPU:1, one launch (start us, length us, event | category | flops | bytes accessed | tf_op | source)
XLA Modules:
  0.0 47.4 jit_solution(138381159378537280)
XLA Ops:
  0.6 45.3 %chain.1 = (f32[2,256,256]{2,1,0:T(8,128)S(1)}, f32[8,128]{1,0:T(8,128)S(1)}) custom-call(f32[2,1,256,256]{3,2,1,0:T(8,128)} %t_hbm.1, f32[2,3,1,256,256]{4,3,2,1,0:T(8,128)} %h_hbm.1, s32[1,2]{1,0:T(1,128)} %bitcast.1), custom_call_target="tpu_custom_call" | custom-call | tf_op jit(solution)/shard_map/chain/pallas_call | solution.py:353
  45.9 1.4 %finish.1 = (f32[2,1,256,256]{3,2,1,0:T(8,128)}, f32[2,3]{1,0:T(2,128)}) custom-call(f32[2,256,256]{2,1,0:T(8,128)S(1)} %get-tuple-element.4.lefts, f32[8,128]{1,0:T(8,128)S(1)} %get-tuple-element.5.sums_ref), custom_call_target="tpu_custom_call" | custom-call | tf_op jit(solution)/shard_map/finish/pallas_call | solution.py:383

commit v4 on v3

--- a/solution.py
+++ b/solution.py
@@ -249,18 +249,15 @@
                 y_copy(direction, step, part)
         if step > 1:
             take_blocks(step - 1)
-    take_blocks(3)
-
-    @pl.when(z < 4)
-    def _():
+
+    def from_lefts():
         lefts_from(acc_p[...])
         whole = mm(left1_ref[...], t[1])
         inner[0] = mm(acc_p[...], whole, TN)
         inner[1] = mm(left1_ref[...], whole, TN)
         inner[2] = mm(whole, whole, TN)
 
-    @pl.when(z >= 4)
-    def _():
+    def from_rights():
         right1 = acc_m[...]
         right0 = mm(t[1], right1)
         whole = mm(t[0], right0)
@@ -268,6 +265,12 @@
         inner[1] = mm(whole, right1, NT)
         inner[2] = mm(whole, whole, NT)
 
+    pl.when(z < 3)(from_lefts)
+    pl.when(z > 4)(from_rights)
+    take_blocks(3)
+    pl.when(z == 3)(from_lefts)
+    pl.when(z == 4)(from_rights)
+
     for part in range(PARTS):
         for direction in range(2):
             z_wait(direction, 4, part)
@@ -330,11 +333,9 @@
 def finish(lefts, sums_ref, left_hbm, energy_ref, sems):
     stores = []
     for c in range(2):
-        for k in range(4):
-            rows = pl.ds(k * QUARTER, QUARTER)
-            copy = pltpu.make_async_copy(lefts.at[c, rows], left_hbm.at[c, 0, rows], sems.at[c, k])
-            copy.start()
-            stores.append(copy)
+        copy = pltpu.make_async_copy(lefts.at[c], left_hbm.at[c, 0], sems.at[c])
+        copy.start()
+        stores.append(copy)
     total = sums_ref[...]
     total = jnp.sum(total, axis=1, keepdims=True)
     values = (float(N * S) * total[0:6]) / total[6:7]
@@ -389,7 +390,7 @@
         ),
         in_specs=[vmem, vmem],
         out_specs=(pl.BlockSpec(memory_space=pl.ANY), vmem),
-        scratch_shapes=[dma((2, 4))],
+        scratch_shapes=[dma((2,))],
     )(*(pltpu.with_memory_space_constraint(x, pltpu.VMEM) for x in (lefts, sums)))
 
 

time: 47.5 us -> 46.4 us (0.977)
  Pallas kernels: 46.7 us -> 45.6 us
    pallas_call x1, Pallas kernels: 45.3 us -> 44.2 us  [per_device(): pl.pallas_call(kernel, name='chain', out_shape=(pltpu.VMEM((2, N, N), F32...]
where the time goes in v4:
time: 46.4 us; the launch traced here: 46.2 us
  Pallas kernels  45.6 us (98%)
  between operations  0.64 us (1%)
    pallas_call x1, Pallas kernels, per_device(): pl.pallas_call(kernel, name='chain', out_shape=(pltpu.VMEM((2, N, N), F32...  44.2 us
    pallas_call x1, Pallas kernels, per_device(): pl.pallas_call(finish, name='finish', out_shape=(jax.ShapeDtypeStruct((2,...  1.37 us

profile of v4, /device:TPU:1, one launch (start us, length us, event | category | flops | bytes accessed | tf_op | source)
XLA Modules:
  0.0 46.2 jit_solution(13910192400185235238)
XLA Ops:
  0.6 44.2 %chain.1 = (f32[2,256,256]{2,1,0:T(8,128)S(1)}, f32[8,128]{1,0:T(8,128)S(1)}) custom-call(f32[2,1,256,256]{3,2,1,0:T(8,128)} %t_hbm.1, f32[2,3,1,256,256]{4,3,2,1,0:T(8,128)} %h_hbm.1, s32[1,2]{1,0:T(1,128)} %bitcast.1), custom_call_target="tpu_custom_call" | custom-call | tf_op jit(solution)/shard_map/chain/pallas_call | solution.py:354
  44.9 1.4 %finish.1 = (f32[2,1,256,256]{3,2,1,0:T(8,128)}, f32[2,3]{1,0:T(2,128)}) custom-call(f32[2,256,256]{2,1,0:T(8,128)S(1)} %get-tuple-element.4.lefts, f32[8,128]{1,0:T(8,128)S(1)} %get-tuple-element.5.sums_ref), custom_call_target="tpu_custom_call" | custom-call | tf_op jit(solution)/shard_map/finish/pallas_call | solution.py:384

commit v5 on v4

--- a/solution.py
+++ b/solution.py
@@ -40,8 +40,8 @@
 def kernel(
     t_hbm, h_hbm, kept_ref,
     lout, sums_ref,
-    t, h, g, r, acc_p, acc_m, post, left1_ref, inner, red,
-    load_sem, g_send, g_recv, z_send, z_recv, y_send, y_recv, s_send, s_recv,
+    t, h, g, r, away, acc_p, acc_m, post, left1_ref, inner, red,
+    load_sem, g_send, g_recv, z_send, z_recv, y_send, y_recv, c_send, c_recv, s_send, s_recv,
 ):
     col = lax.axis_index("col")
     sec = lax.axis_index("sec")
@@ -62,16 +62,18 @@
     loads[1].start()
 
     barrier = pltpu.get_barrier_semaphore()
-    partners = [(at_y(1), sec), (at_y(-1), sec), (at_z(1), sec), (at_z(-1), sec)]
+    other = sec + 1 - 2 * lax.rem(sec, 2)
+    partners = [(at_y(1), sec), (at_y(-1), sec), (at_y(1), other), (at_y(-1), other)]
+    partners += [(at_z(1), other), (at_z(-1), other)]
     partners += [(col, lax.rem(sec + d, S)) for d in range(1, S)]
     for partner in partners:
         pl.semaphore_signal(barrier, inc=1, device_id=partner, device_id_type=MESH)
 
     sends = []
 
-    def send(ref, target, send_sem, recv_sem):
+    def send(ref, target, send_sem, recv_sem, to=None):
         copy = pltpu.make_async_remote_copy(
-            src_ref=ref, dst_ref=ref, send_sem=send_sem, recv_sem=recv_sem,
+            src_ref=ref, dst_ref=ref if to is None else to, send_sem=send_sem, recv_sem=recv_sem,
             device_id=target, device_id_type=MESH,
         )
         copy.start()
@@ -92,7 +94,7 @@
     pl.semaphore_wait(barrier, len(partners))
 
     y_plus, y_minus = (at_y(1), sec), (at_y(-1), sec)
-    z_plus, z_minus = (at_z(1), sec), (at_z(-1), sec)
+    z_plus, z_minus = (at_z(1), other), (at_z(-1), other)
     before, after, opposite = lax.rem(y + 3, Y), lax.rem(y + 1, Y), lax.rem(y + 2, Y)
 
     def g_rows(direction, index):
@@ -155,18 +157,33 @@
         return lax.rem(z - step + Z, Z) if direction == 0 else lax.rem(z + step, Z)
 
     def z_copy(direction, step, part):
-        ref = r.at[z_block(direction, step - 1), chunk(direction, part)]
+        place = (z_block(direction, step - 1), chunk(direction, part))
         target = z_plus if direction == 0 else z_minus
-        send(ref, target, z_send.at[direction, step - 1, part], z_recv.at[direction, step - 1, part])
+        here, there = (r, away) if step % 2 else (away, r)
+        index = (direction, step - 1, part)
+        send(here.at[place], target, z_send.at[index], z_recv.at[index], there.at[place])
 
     def z_wait(direction, step, part):
-        ref = r.at[z_block(direction, step), chunk(direction, part)]
-        arrived(ref, z_send.at[direction, step - 1, part], z_recv.at[direction, step - 1, part])
+        ref = (away if step % 2 else r).at[z_block(direction, step), chunk(direction, part)]
+        index = (direction, step - 1, part)
+        arrived(ref, z_send.at[index], z_recv.at[index])
 
     def y_copy(direction, step, part):
-        ref = r.at[z_block(direction, step), chunk(direction, part)]
-        target = y_plus if part < PARTS // 2 else y_minus
-        send(ref, target, y_send.at[direction, step - 1, part], y_recv.at[direction, step - 1, part])
+        place = (z_block(direction, step), chunk(direction, part))
+        owner = other if step % 2 else sec
+        target = (at_y(1 if part < PARTS // 2 else -1), owner)
+        index = (direction, step - 1, part)
+        here = away if step % 2 else r
+        send(here.at[place], target, y_send.at[index], y_recv.at[index], r.at[place])
+
+    def c_copy(direction, step, part):
+        place = (z_block(direction, step), chunk(direction, part))
+        index = (direction, step // 2, part)
+        send(away.at[place], (col, other), c_send.at[index], c_recv.at[index], r.at[place])
+
+    def c_wait(direction, step, part):
+        index = (direction, step // 2, part)
+        arrived(r.at[z_block(direction, step), chunk(direction, part)], c_send.at[index], c_recv.at[index])
 
     def y_wait(direction, step, part):
         shift = 3 * QUARTER if part < PARTS // 2 else QUARTER
@@ -213,6 +230,8 @@
     def take_blocks(step):
         for direction in range(2):
             for part in range(PARTS):
+                if step % 2:
+                    c_wait(direction, step, part)
                 y_wait(direction, step, part)
         plus = z_block(0, step)
         minus = z_block(1, step)
@@ -247,6 +266,8 @@
                 z_wait(direction, step, part)
                 z_copy(direction, step + 1, part)
                 y_copy(direction, step, part)
+                if step % 2:
+                    c_copy(direction, step, part)
         if step > 1:
             take_blocks(step - 1)
 
@@ -366,6 +387,7 @@
             pltpu.VMEM((2, TERMS, N, N), F32),
             pltpu.VMEM((Y, N, N), F32),
             pltpu.VMEM((Z, N, N), F32),
+            pltpu.VMEM((Z, N, N), F32),
             *[pltpu.VMEM((N, N), F32)] * 4,
             pltpu.VMEM((3, N, N), F32),
             pltpu.VMEM((S, 8, 128), F32),
@@ -376,6 +398,8 @@
             dma((2, 4, PARTS)),
             dma((2, 3, PARTS)),
             dma((2, 3, PARTS)),
+            dma((2, 2, PARTS)),
+            dma((2, 2, PARTS)),
             dma((S,)),
             dma((S,)),
         ],

time: 46.4 us -> 46 us (level)
  no operation moved by 1% of the time
where the time goes in v5:
time: 46 us; the launch traced here: 45.8 us
  Pallas kernels  45.2 us (98%)
  between operations  0.64 us (1%)
    pallas_call x1, Pallas kernels, per_device(): pl.pallas_call(kernel, name='chain', out_shape=(pltpu.VMEM((2, N, N), F32...  43.8 us
    pallas_call x1, Pallas kernels, per_device(): pl.pallas_call(finish, name='finish', out_shape=(jax.ShapeDtypeStruct((2,...  1.37 us

profile of v5, /device:TPU:1, one launch (start us, length us, event | category | flops | bytes accessed | tf_op | source)
XLA Modules:
  0.0 45.8 jit_solution(6817147907604901268)
XLA Ops:
  0.6 43.8 %chain.1 = (f32[2,256,256]{2,1,0:T(8,128)S(1)}, f32[8,128]{1,0:T(8,128)S(1)}) custom-call(f32[2,1,256,256]{3,2,1,0:T(8,128)} %t_hbm.1, f32[2,3,1,256,256]{4,3,2,1,0:T(8,128)} %h_hbm.1, s32[1,2]{1,0:T(1,128)} %bitcast.1), custom_call_target="tpu_custom_call" | custom-call | tf_op jit(solution)/shard_map/chain/pallas_call | solution.py:375
  44.5 1.4 %finish.1 = (f32[2,1,256,256]{3,2,1,0:T(8,128)}, f32[2,3]{1,0:T(2,128)}) custom-call(f32[2,256,256]{2,1,0:T(8,128)S(1)} %get-tuple-element.4.lefts, f32[8,128]{1,0:T(8,128)S(1)} %get-tuple-element.5.sums_ref), custom_call_target="tpu_custom_call" | custom-call | tf_op jit(solution)/shard_map/finish/pallas_call | solution.py:408

commit v6 on v5

--- a/solution.py
+++ b/solution.py
@@ -40,7 +40,7 @@
 def kernel(
     t_hbm, h_hbm, kept_ref,
     lout, sums_ref,
-    t, h, g, r, away, acc_p, acc_m, post, left1_ref, inner, red,
+    t, h, g, r, away, acc_p, acc_m, post, factor, q, red,
     load_sem, g_send, g_recv, z_send, z_recv, y_send, y_recv, c_send, c_recv, s_send, s_recv,
 ):
     col = lax.axis_index("col")
@@ -221,9 +221,7 @@
     def _():
         acc_m[...] = (row == column).astype(F32)
 
-    def lefts_from(left0):
-        left1 = mm(left0, t[0])
-        left1_ref[...] = left1
+    def write_lefts(left0, left1):
         lout[0] = jnp.where(column < kept_ref[0, 0], left0, 0.0)
         lout[1] = jnp.where(column < kept_ref[0, 1], left1, 0.0)
 
@@ -236,7 +234,7 @@
         plus = z_block(0, step)
         minus = z_block(1, step)
 
-        @pl.when(step <= z)
+        @pl.when(step <= z - step // 3)
         def _():
             acc_p[...] = mm(r[plus], acc_p[...])
 
@@ -248,7 +246,7 @@
         def _():
             post[...] = mm(r[plus], post[...])
 
-        @pl.when(step <= Z - 1 - z)
+        @pl.when(step <= Z - 1 - z - step // 3)
         def _():
             acc_m[...] = mm(acc_m[...], r[minus])
 
@@ -271,26 +269,40 @@
         if step > 1:
             take_blocks(step - 1)
 
-    def from_lefts():
-        lefts_from(acc_p[...])
-        whole = mm(left1_ref[...], t[1])
-        inner[0] = mm(acc_p[...], whole, TN)
-        inner[1] = mm(left1_ref[...], whole, TN)
-        inner[2] = mm(whole, whole, TN)
-
-    def from_rights():
-        right1 = acc_m[...]
-        right0 = mm(t[1], right1)
-        whole = mm(t[0], right0)
-        inner[0] = mm(whole, right0, NT)
-        inner[1] = mm(whole, right1, NT)
-        inner[2] = mm(whole, whole, NT)
-
-    pl.when(z < 3)(from_lefts)
-    pl.when(z > 4)(from_rights)
+    @pl.when(z < 4)
+    def _():
+        x0 = acc_p[...]
+        x1 = mm(x0, t[0])
+        x2 = mm(x1, t[1])
+        q[6] = x2
+        factor[...] = x2
+        for k in range(TERMS):
+            q[k] = mm(x0, h[0, k])
+            q[3 + k] = mm(x1, h[1, k])
+        write_lefts(x0, x1)
+
+    @pl.when(z >= 4)
+    def _():
+        x0 = acc_m[...]
+        x1 = mm(t[1], x0)
+        x2 = mm(t[0], x1)
+        q[6] = x2
+        factor[...] = x2
+        for k in range(TERMS):
+            q[k] = mm(h[0, k], x1)
+            q[3 + k] = mm(h[1, k], x0)
+
     take_blocks(3)
-    pl.when(z == 3)(from_lefts)
-    pl.when(z == 4)(from_rights)
+
+    @pl.when(z == 3)
+    def _():
+        block = r[0]
+        factor[...] = mm(block, mm(block, factor[...]), TN)
+
+    @pl.when(z == 4)
+    def _():
+        block = r[Z - 1]
+        factor[...] = mm(mm(factor[...], block), block, NT)
 
     for part in range(PARTS):
         for direction in range(2):
@@ -317,28 +329,31 @@
         x = jnp.sum(x, axis=0, keepdims=True)
         return x[:, :128] + x[:, 128:]
 
-    def reduce(inner0, inner1, gram):
-        rows = [lanes(inner0 * h[0, k]) for k in range(TERMS)]
-        rows += [lanes(inner1 * h[1, k]) for k in range(TERMS)]
-        rows += [lanes(inner[2] * gram), jnp.zeros((1, 128), F32)]
+    def reduce(v):
+        rows = [lanes(v * q[k]) for k in range(7)] + [jnp.zeros((1, 128), F32)]
         red[sec] = jnp.concatenate(rows, axis=0)
 
     @pl.when(z < 4)
     def _():
         gram = mm(acc_m[...], acc_m[...], NT)
-        reduce(mm(inner[0], gram), mm(inner[1], gram), gram)
+        reduce(mm(factor[...], gram))
 
     @pl.when(z >= 4)
     def _():
         gram = mm(acc_p[...], acc_p[...], TN)
-        reduce(mm(gram, inner[0]), mm(gram, inner[1]), gram)
+        reduce(mm(gram, factor[...]))
 
     for d in (4, 3, 5, 2, 6, 1, 7):
         send(red.at[sec], (col, lax.rem(sec + d, S)), s_send.at[d], s_recv.at[d])
 
+    @pl.when(z == 3)
+    def _():
+        left0 = mm(r[0], acc_p[...])
+        write_lefts(left0, mm(left0, t[0]))
+
     @pl.when(z >= 4)
     def _():
-        lefts_from(acc_p[...])
+        write_lefts(acc_p[...], mm(acc_p[...], t[0]))
 
     for d in range(1, S):
         arrived(red.at[lax.rem(sec - d + S, S)], s_send.at[d], s_recv.at[d])
@@ -389,7 +404,7 @@
             pltpu.VMEM((Z, N, N), F32),
             pltpu.VMEM((Z, N, N), F32),
             *[pltpu.VMEM((N, N), F32)] * 4,
-            pltpu.VMEM((3, N, N), F32),
+            pltpu.VMEM((7, N, N), F32),
             pltpu.VMEM((S, 8, 128), F32),
             dma((3,)),
             dma((2, 6)),

time: 46 us -> 45.9 us (level)
  no operation moved by 1% of the time
where the time goes in v6:
time: 45.9 us; the launch traced here: 45.7 us
  Pallas kernels  45.1 us (98%)
  between operations  0.64 us (1%)
    pallas_call x1, Pallas kernels, per_device(): pl.pallas_call(kernel, name='chain', out_shape=(pltpu.VMEM((2, N, N), F32...  43.7 us
    pallas_call x1, Pallas kernels, per_device(): pl.pallas_call(finish, name='finish', out_shape=(jax.ShapeDtypeStruct((2,...  1.37 us

profile of v6, /device:TPU:1, one launch (start us, length us, event | category | flops | bytes accessed | tf_op | source)
XLA Modules:
  0.0 45.7 jit_solution(549584606808814092)
XLA Ops:
  0.6 43.7 %chain.1 = (f32[2,256,256]{2,1,0:T(8,128)S(1)}, f32[8,128]{1,0:T(8,128)S(1)}) custom-call(f32[2,1,256,256]{3,2,1,0:T(8,128)} %t_hbm.1, f32[2,3,1,256,256]{4,3,2,1,0:T(8,128)} %h_hbm.1, s32[1,2]{1,0:T(1,128)} %bitcast.1), custom_call_target="tpu_custom_call" | custom-call | tf_op jit(solution)/shard_map/chain/pallas_call | solution.py:390
  44.4 1.4 %finish.1 = (f32[2,1,256,256]{3,2,1,0:T(8,128)}, f32[2,3]{1,0:T(2,128)}) custom-call(f32[2,256,256]{2,1,0:T(8,128)S(1)} %get-tuple-element.4.lefts, f32[8,128]{1,0:T(8,128)S(1)} %get-tuple-element.5.sums_ref), custom_call_target="tpu_custom_call" | custom-call | tf_op jit(solution)/shard_map/finish/pallas_call | solution.py:423

commit v7 on v6

--- a/solution.py
+++ b/solution.py
@@ -171,7 +171,7 @@
     def y_copy(direction, step, part):
         place = (z_block(direction, step), chunk(direction, part))
         owner = other if step % 2 else sec
-        target = (at_y(1 if part < PARTS // 2 else -1), owner)
+        target = (at_y(1 - 2 * (part // (PARTS // 2))), owner)
         index = (direction, step - 1, part)
         here = away if step % 2 else r
         send(here.at[place], target, y_send.at[index], y_recv.at[index], r.at[place])
@@ -190,7 +190,8 @@
         ref = r.at[z_block(direction, step), chunk(direction, part, shift)]
         arrived(ref, y_send.at[direction, step - 1, part], y_recv.at[direction, step - 1, part])
 
-    for part in range(PARTS):
+    order = [lax.rem(part + (PARTS // 2) * ((Y - 1 - y) // (Y - 1)), PARTS) for part in range(PARTS)]
+    for part in order:
         for direction in range(2):
             z_copy(direction, 1, part)
 
@@ -259,7 +260,7 @@
             post[...] = mm(post[...], r[minus])
 
     for step in range(1, 4):
-        for part in range(PARTS):
+        for part in order:
             for direction in range(2):
                 z_wait(direction, step, part)
                 z_copy(direction, step + 1, part)

time: 45.9 us -> 45.7 us (level)
  no operation moved by 1% of the time
where the time goes in v7:
time: 45.7 us; the launch traced here: 45.6 us
  Pallas kernels  45 us (98%)
  between operations  0.64 us (1%)
    pallas_call x1, Pallas kernels, per_device(): pl.pallas_call(kernel, name='chain', out_shape=(pltpu.VMEM((2, N, N), F32...  43.6 us
    pallas_call x1, Pallas kernels, per_device(): pl.pallas_call(finish, name='finish', out_shape=(jax.ShapeDtypeStruct((2,...  1.37 us

profile of v7, /device:TPU:1, one launch (start us, length us, event | category | flops | bytes accessed | tf_op | source)
XLA Modules:
  0.0 45.6 jit_solution(5298572062879111551)
XLA Ops:
  0.6 43.6 %chain.1 = (f32[2,256,256]{2,1,0:T(8,128)S(1)}, f32[8,128]{1,0:T(8,128)S(1)}) custom-call(f32[2,1,256,256]{3,2,1,0:T(8,128)} %t_hbm.1, f32[2,3,1,256,256]{4,3,2,1,0:T(8,128)} %h_hbm.1, s32[1,2]{1,0:T(1,128)} %bitcast.1), custom_call_target="tpu_custom_call" | custom-call | tf_op jit(solution)/shard_map/chain/pallas_call | solution.py:391
  44.2 1.4 %finish.1 = (f32[2,1,256,256]{3,2,1,0:T(8,128)}, f32[2,3]{1,0:T(2,128)}) custom-call(f32[2,256,256]{2,1,0:T(8,128)S(1)} %get-tuple-element.4.lefts, f32[8,128]{1,0:T(8,128)S(1)} %get-tuple-element.5.sums_ref), custom_call_target="tpu_custom_call" | custom-call | tf_op jit(solution)/shard_map/finish/pallas_call | solution.py:424

commit v8 on v6

--- a/solution.py
+++ b/solution.py
@@ -14,8 +14,8 @@
 N = 256
 HALF = N // 2
 QUARTER = N // 4
-PARTS = 4
-ROWS = HALF // PARTS
+SIZES = ((64,), (40, 24))
+PARTS = [(half, sum(sizes[:k]), sizes[k]) for half, sizes in enumerate(SIZES) for k in range(len(sizes))]
 TERMS = 3
 NN = (((1,), (0,)), ((), ()))
 NT = (((1,), (1,)), ((), ()))
@@ -141,17 +141,37 @@
     for index in range(2, 4):
         for direction in range(2):
             g_wait(direction, index, neighbours[direction])
+
+    @pl.when(y < 2)
+    def _():
+        acc_p[...] = mm(g[0], g[1])
+
+    @pl.when(y >= 2)
+    def _():
+        acc_m[...] = mm(g[2], g[3])
+
     for index in range(4, 6):
         for direction in range(2):
             g_wait(direction, index, opposite)
 
-    low = mm(g[0], g[1])
-    high = mm(g[2], g[3])
-    r[z] = mm(low, high)
-
-    def chunk(direction, part, shift=0):
-        start = lax.rem(y * QUARTER + direction * HALF + part * ROWS + shift, N)
-        return pl.ds(pl.multiple_of(start, ROWS), ROWS)
+    @pl.when(y < 2)
+    def _():
+        acc_m[...] = mm(g[2], g[3])
+
+    @pl.when(y >= 2)
+    def _():
+        acc_p[...] = mm(g[0], g[1])
+
+    r[z] = mm(acc_p[...], acc_m[...])
+
+    flip = (Y - 1 - y) // (Y - 1)
+
+    def rows_at(start, size):
+        return pl.ds(pl.multiple_of(lax.rem(y * QUARTER + start, N), 8), size)
+
+    def chunk(direction, part):
+        half, offset, size = PARTS[part]
+        return rows_at(direction * HALF + lax.rem(half + flip, 2) * QUARTER + offset, size)
 
     def z_block(direction, step):
         return lax.rem(z - step + Z, Z) if direction == 0 else lax.rem(z + step, Z)
@@ -171,31 +191,31 @@
     def y_copy(direction, step, part):
         place = (z_block(direction, step), chunk(direction, part))
         owner = other if step % 2 else sec
-        target = (at_y(1 if part < PARTS // 2 else -1), owner)
-        index = (direction, step - 1, part)
+        quarter = lax.rem(PARTS[part][0] + flip, 2)
+        target = (at_y(1 - 2 * quarter), owner)
         here = away if step % 2 else r
-        send(here.at[place], target, y_send.at[index], y_recv.at[index], r.at[place])
-
-    def c_copy(direction, step, part):
-        place = (z_block(direction, step), chunk(direction, part))
-        index = (direction, step // 2, part)
+        send(here.at[place], target, y_send.at[direction, step - 1, part], y_recv.at[direction, step - 1, quarter], r.at[place])
+
+    def quarter_rows(direction, half):
+        return rows_at(direction * HALF + lax.rem(half + flip, 2) * QUARTER, QUARTER)
+
+    def c_copy(direction, step, half):
+        place = (z_block(direction, step), quarter_rows(direction, half))
+        index = (direction, step // 2, half)
         send(away.at[place], (col, other), c_send.at[index], c_recv.at[index], r.at[place])
 
-    def c_wait(direction, step, part):
-        index = (direction, step // 2, part)
-        arrived(r.at[z_block(direction, step), chunk(direction, part)], c_send.at[index], c_recv.at[index])
-
-    def y_wait(direction, step, part):
-        shift = 3 * QUARTER if part < PARTS // 2 else QUARTER
-        ref = r.at[z_block(direction, step), chunk(direction, part, shift)]
-        arrived(ref, y_send.at[direction, step - 1, part], y_recv.at[direction, step - 1, part])
-
-    for part in range(PARTS):
+    def c_wait(direction, step, half):
+        index = (direction, step // 2, half)
+        arrived(r.at[z_block(direction, step), quarter_rows(direction, half)], c_send.at[index], c_recv.at[index])
+
+    def y_wait(direction, step, quarter):
+        rows = rows_at(direction * HALF + (3 - quarter) * QUARTER, QUARTER)
+        index = (direction, step - 1, quarter)
+        arrived(r.at[z_block(direction, step), rows], y_send.at[direction, step - 1, 0], y_recv.at[index])
+
+    for part in range(len(PARTS)):
         for direction in range(2):
             z_copy(direction, 1, part)
-
-    acc_p[...] = low
-    acc_m[...] = high
 
     @pl.when(y == 0)
     def _():
@@ -227,10 +247,11 @@
 
     def take_blocks(step):
         for direction in range(2):
-            for part in range(PARTS):
-                if step % 2:
-                    c_wait(direction, step, part)
-                y_wait(direction, step, part)
+            if step % 2:
+                for half in range(2):
+                    c_wait(direction, step, half)
+            for quarter in range(2):
+                y_wait(direction, step, quarter)
         plus = z_block(0, step)
         minus = z_block(1, step)
 
@@ -259,13 +280,13 @@
             post[...] = mm(post[...], r[minus])
 
     for step in range(1, 4):
-        for part in range(PARTS):
+        for part in range(len(PARTS)):
             for direction in range(2):
                 z_wait(direction, step, part)
                 z_copy(direction, step + 1, part)
                 y_copy(direction, step, part)
-                if step % 2:
-                    c_copy(direction, step, part)
+                if step % 2 and sum(PARTS[part][1:]) == QUARTER:
+                    c_copy(direction, step, PARTS[part][0])
         if step > 1:
             take_blocks(step - 1)
 
@@ -304,7 +325,7 @@
         block = r[Z - 1]
         factor[...] = mm(mm(factor[...], block), block, NT)
 
-    for part in range(PARTS):
+    for part in range(len(PARTS)):
         for direction in range(2):
             z_wait(direction, 4, part)
     middle = lax.rem(z + 4, Z)
@@ -409,12 +430,12 @@
             dma((3,)),
             dma((2, 6)),
             dma((2, 6)),
-            dma((2, 4, PARTS)),
-            dma((2, 4, PARTS)),
-            dma((2, 3, PARTS)),
-            dma((2, 3, PARTS)),
-            dma((2, 2, PARTS)),
-            dma((2, 2, PARTS)),
+            dma((2, 4, len(PARTS))),
+            dma((2, 4, len(PARTS))),
+            dma((2, 3, len(PARTS))),
+            dma((2, 3, 2)),
+            dma((2, 2, len(PARTS))),
+            dma((2, 2, len(PARTS))),
             dma((S,)),
             dma((S,)),
         ],

time: 45.9 us -> 45.7 us (level)
  no operation moved by 1% of the time
where the time goes in v8:
time: 45.7 us; the launch traced here: 45.6 us
  Pallas kernels  45 us (98%)
  between operations  0.64 us (1%)
    pallas_call x1, Pallas kernels, per_device(): pl.pallas_call(kernel, name='chain', out_shape=(pltpu.VMEM((2, N, N), F32...  43.6 us
    pallas_call x1, Pallas kernels, per_device(): pl.pallas_call(finish, name='finish', out_shape=(jax.ShapeDtypeStruct((2,...  1.37 us

profile of v8, /device:TPU:1, one launch (start us, length us, event | category | flops | bytes accessed | tf_op | source)
XLA Modules:
  0.0 45.6 jit_solution(8079540498906517279)
XLA Ops:
  0.6 43.6 %chain.1 = (f32[2,256,256]{2,1,0:T(8,128)S(1)}, f32[8,128]{1,0:T(8,128)S(1)}) custom-call(f32[2,1,256,256]{3,2,1,0:T(8,128)} %t_hbm.1, f32[2,3,1,256,256]{4,3,2,1,0:T(8,128)} %h_hbm.1, s32[1,2]{1,0:T(1,128)} %bitcast.1), custom_call_target="tpu_custom_call" | custom-call | tf_op jit(solution)/shard_map/chain/pallas_call | solution.py:411
  44.2 1.4 %finish.1 = (f32[2,1,256,256]{3,2,1,0:T(8,128)}, f32[2,3]{1,0:T(2,128)}) custom-call(f32[2,256,256]{2,1,0:T(8,128)S(1)} %get-tuple-element.4.lefts, f32[8,128]{1,0:T(8,128)S(1)} %get-tuple-element.5.sums_ref), custom_call_target="tpu_custom_call" | custom-call | tf_op jit(solution)/shard_map/finish/pallas_call | solution.py:444

commit v9 on v8

--- a/solution.py
+++ b/solution.py
@@ -14,6 +14,8 @@
 N = 256
 HALF = N // 2
 QUARTER = N // 4
+BASE = 104
+CUTS = ((0, BASE), (BASE, N - 2 * BASE), (N - BASE, BASE))
 SIZES = ((64,), (40, 24))
 PARTS = [(half, sum(sizes[:k]), sizes[k]) for half, sizes in enumerate(SIZES) for k in range(len(sizes))]
 TERMS = 3
@@ -98,22 +100,21 @@
     before, after, opposite = lax.rem(y + 3, Y), lax.rem(y + 1, Y), lax.rem(y + 2, Y)
 
     def g_rows(direction, index):
-        part = (index + 2 * direction) % 4
-        return pl.ds(part * QUARTER, QUARTER)
+        start, size = CUTS[index if direction == 0 else 2 - index]
+        return pl.ds(start, size)
 
     def g_copy(direction, index, block):
         target = y_plus if direction == 0 else y_minus
-        rows = g_rows(direction, index % 4)
+        rows = g_rows(direction, index % 3)
         send(g.at[block, rows], target, g_send.at[direction, index], g_recv.at[direction, index])
 
     def g_wait(direction, index, block):
-        rows = g_rows(direction, index % 4)
+        rows = g_rows(direction, index % 3)
         arrived(g.at[block, rows], g_send.at[direction, index], g_recv.at[direction, index])
 
     g_copy(0, 0, y)
-    g_copy(0, 1, y)
     g[y, bottom] = mm(t[0, bottom], t[1])
-    for direction, index in ((1, 0), (1, 1), (0, 2), (1, 2), (0, 3), (1, 3)):
+    for direction, index in ((1, 0), (0, 1), (1, 1), (0, 2), (1, 2)):
         g_copy(direction, index, y)
 
     loads[2].wait()
@@ -134,13 +135,21 @@
             h[1, k] = mm(t[0], h[1, k])
 
     neighbours = (before, after)
-    for index in range(2):
+    inside = lax.rem(y, Y - 1) != 0
+    for direction in range(2):
+        g_wait(direction, 0, neighbours[direction])
+        g_copy(direction, 3, neighbours[direction])
+    for direction in range(2):
+        g_wait(direction, 1, neighbours[direction])
+
+    @pl.when(inside)
+    def _():
         for direction in range(2):
-            g_wait(direction, index, neighbours[direction])
-            g_copy(direction, index + 4, neighbours[direction])
-    for index in range(2, 4):
-        for direction in range(2):
-            g_wait(direction, index, neighbours[direction])
+            g_copy(direction, 4, neighbours[direction])
+            sends.pop()
+
+    for direction in range(2):
+        g_wait(direction, 2, neighbours[direction])
 
     @pl.when(y < 2)
     def _():
@@ -150,9 +159,16 @@
     def _():
         acc_m[...] = mm(g[2], g[3])
 
-    for index in range(4, 6):
-        for direction in range(2):
-            g_wait(direction, index, opposite)
+    for direction in range(2):
+        g_wait(direction, 3, opposite)
+
+    @pl.when(y < 2)
+    def _():
+        g_wait(1, 4, opposite)
+
+    @pl.when(y >= 2)
+    def _():
+        g_wait(0, 4, opposite)
 
     @pl.when(y < 2)
     def _():
@@ -385,6 +401,15 @@
 
     for copy in sends:
         copy.wait_send()
+
+    @pl.when(inside)
+    def _():
+        for direction in range(2):
+            ref = g.at[neighbours[direction], g_rows(direction, 1)]
+            pltpu.make_async_remote_copy(
+                src_ref=ref, dst_ref=ref, send_sem=g_send.at[direction, 4], recv_sem=g_recv.at[direction, 4],
+                device_id=y_plus, device_id_type=MESH,
+            ).wait_send()
 
 
 def finish(lefts, sums_ref, left_hbm, energy_ref, sems):
@@ -428,8 +453,8 @@
             pltpu.VMEM((7, N, N), F32),
             pltpu.VMEM((S, 8, 128), F32),
             dma((3,)),
-            dma((2, 6)),
-            dma((2, 6)),
+            dma((2, 5)),
+            dma((2, 5)),
             dma((2, 4, len(PARTS))),
             dma((2, 4, len(PARTS))),
             dma((2, 3, len(PARTS))),

time: 45.7 us -> 45.4 us (level)
  no operation moved by 1% of the time
where the time goes in v9:
time: 45.4 us; the launch traced here: 45.2 us
  Pallas kernels  44.6 us (98%)
  between operations  0.64 us (1%)
    pallas_call x1, Pallas kernels, per_device(): pl.pallas_call(kernel, name='chain', out_shape=(pltpu.VMEM((2, N, N), F32...  43.2 us
    pallas_call x1, Pallas kernels, per_device(): pl.pallas_call(finish, name='finish', out_shape=(jax.ShapeDtypeStruct((2,...  1.37 us

profile of v9, /device:TPU:1, one launch (start us, length us, event | category | flops | bytes accessed | tf_op | source)
XLA Modules:
  0.0 45.2 jit_solution(3527962675823247829)
XLA Ops:
  0.6 43.2 %chain.1 = (f32[2,256,256]{2,1,0:T(8,128)S(1)}, f32[8,128]{1,0:T(8,128)S(1)}) custom-call(f32[2,1,256,256]{3,2,1,0:T(8,128)} %t_hbm.1, f32[2,3,1,256,256]{4,3,2,1,0:T(8,128)} %h_hbm.1, s32[1,2]{1,0:T(1,128)} %bitcast.1), custom_call_target="tpu_custom_call" | custom-call | tf_op jit(solution)/shard_map/chain/pallas_call | solution.py:436
  43.9 1.4 %finish.1 = (f32[2,1,256,256]{3,2,1,0:T(8,128)}, f32[2,3]{1,0:T(2,128)}) custom-call(f32[2,256,256]{2,1,0:T(8,128)S(1)} %get-tuple-element.4.lefts, f32[8,128]{1,0:T(8,128)S(1)} %get-tuple-element.5.sums_ref), custom_call_target="tpu_custom_call" | custom-call | tf_op jit(solution)/shard_map/finish/pallas_call | solution.py:469

commit v10 on v9

--- a/solution.py
+++ b/solution.py
@@ -303,8 +303,9 @@
                 y_copy(direction, step, part)
                 if step % 2 and sum(PARTS[part][1:]) == QUARTER:
                     c_copy(direction, step, PARTS[part][0])
-        if step > 1:
-            take_blocks(step - 1)
+        if step == 3:
+            take_blocks(1)
+            take_blocks(2)
 
     @pl.when(z < 4)
     def _():

time: 45.4 us -> 45.4 us (level)
  no operation moved by 1% of the time
where the time goes in v10:
time: 45.4 us; the launch traced here: 45.2 us
  Pallas kernels  44.6 us (98%)
  between operations  0.64 us (1%)
    pallas_call x1, Pallas kernels, per_device(): pl.pallas_call(kernel, name='chain', out_shape=(pltpu.VMEM((2, N, N), F32...  43.2 us
    pallas_call x1, Pallas kernels, per_device(): pl.pallas_call(finish, name='finish', out_shape=(jax.ShapeDtypeStruct((2,...  1.37 us

profile of v10, /device:TPU:1, one launch (start us, length us, event | category | flops | bytes accessed | tf_op | source)
XLA Modules:
  0.0 45.2 jit_solution(3089435510171239726)
XLA Ops:
  0.6 43.2 %chain.1 = (f32[2,256,256]{2,1,0:T(8,128)S(1)}, f32[8,128]{1,0:T(8,128)S(1)}) custom-call(f32[2,1,256,256]{3,2,1,0:T(8,128)} %t_hbm.1, f32[2,3,1,256,256]{4,3,2,1,0:T(8,128)} %h_hbm.1, s32[1,2]{1,0:T(1,128)} %bitcast.1), custom_call_target="tpu_custom_call" | custom-call | tf_op jit(solution)/shard_map/chain/pallas_call | solution.py:437
  43.9 1.4 %finish.1 = (f32[2,1,256,256]{3,2,1,0:T(8,128)}, f32[2,3]{1,0:T(2,128)}) custom-call(f32[2,256,256]{2,1,0:T(8,128)S(1)} %get-tuple-element.4.lefts, f32[8,128]{1,0:T(8,128)S(1)} %get-tuple-element.5.sums_ref), custom_call_target="tpu_custom_call" | custom-call | tf_op jit(solution)/shard_map/finish/pallas_call | solution.py:470

commit v11 on v9

--- a/solution.py
+++ b/solution.py
@@ -392,24 +392,24 @@
     def _():
         write_lefts(acc_p[...], mm(acc_p[...], t[0]))
 
+    for copy in sends:
+        copy.wait_send()
+
+    @pl.when(inside)
+    def _():
+        for direction in range(2):
+            ref = g.at[neighbours[direction], g_rows(direction, 1)]
+            pltpu.make_async_remote_copy(
+                src_ref=ref, dst_ref=ref, send_sem=g_send.at[direction, 4], recv_sem=g_recv.at[direction, 4],
+                device_id=y_plus, device_id_type=MESH,
+            ).wait_send()
+
     for d in range(1, S):
         arrived(red.at[lax.rem(sec - d + S, S)], s_send.at[d], s_recv.at[d])
     total = red[0]
     for k in range(1, S):
         total = total + red[k]
     sums_ref[...] = total
-
-    for copy in sends:
-        copy.wait_send()
-
-    @pl.when(inside)
-    def _():
-        for direction in range(2):
-            ref = g.at[neighbours[direction], g_rows(direction, 1)]
-            pltpu.make_async_remote_copy(
-                src_ref=ref, dst_ref=ref, send_sem=g_send.at[direction, 4], recv_sem=g_recv.at[direction, 4],
-                device_id=y_plus, device_id_type=MESH,
-            ).wait_send()
 
 
 def finish(lefts, sums_ref, left_hbm, energy_ref, sems):

time: 45.4 us -> 45.3 us (level)
  no operation moved by 1% of the time
where the time goes in v11:
time: 45.3 us; the launch traced here: 45.1 us
  Pallas kernels  44.5 us (98%)
  between operations  0.64 us (1%)
    pallas_call x1, Pallas kernels, per_device(): pl.pallas_call(kernel, name='chain', out_shape=(pltpu.VMEM((2, N, N), F32...  43.1 us
    pallas_call x1, Pallas kernels, per_device(): pl.pallas_call(finish, name='finish', out_shape=(jax.ShapeDtypeStruct((2,...  1.37 us

profile of v11, /device:TPU:1, one launch (start us, length us, event | category | flops | bytes accessed | tf_op | source)
XLA Modules:
  0.0 45.1 jit_solution(5787365622187206287)
XLA Ops:
  0.6 43.1 %chain.1 = (f32[2,256,256]{2,1,0:T(8,128)S(1)}, f32[8,128]{1,0:T(8,128)S(1)}) custom-call(f32[2,1,256,256]{3,2,1,0:T(8,128)} %t_hbm.1, f32[2,3,1,256,256]{4,3,2,1,0:T(8,128)} %h_hbm.1, s32[1,2]{1,0:T(1,128)} %bitcast.1), custom_call_target="tpu_custom_call" | custom-call | tf_op jit(solution)/shard_map/chain/pallas_call | solution.py:436
  43.8 1.4 %finish.1 = (f32[2,1,256,256]{3,2,1,0:T(8,128)}, f32[2,3]{1,0:T(2,128)}) custom-call(f32[2,256,256]{2,1,0:T(8,128)S(1)} %get-tuple-element.4.lefts, f32[8,128]{1,0:T(8,128)S(1)} %get-tuple-element.5.sums_ref), custom_call_target="tpu_custom_call" | custom-call | tf_op jit(solution)/shard_map/finish/pallas_call | solution.py:469

commit v12 on v11

--- a/solution.py
+++ b/solution.py
@@ -16,7 +16,7 @@
 QUARTER = N // 4
 BASE = 104
 CUTS = ((0, BASE), (BASE, N - 2 * BASE), (N - BASE, BASE))
-SIZES = ((64,), (40, 24))
+SIZES = ((64,), (64,))
 PARTS = [(half, sum(sizes[:k]), sizes[k]) for half, sizes in enumerate(SIZES) for k in range(len(sizes))]
 TERMS = 3
 NN = (((1,), (0,)), ((), ()))

time: 45.3 us -> 46 us (1.015)
  Pallas kernels: 44.5 us -> 45.2 us
    pallas_call x1, Pallas kernels: 43.1 us -> 43.8 us  [per_device(): pl.pallas_call(kernel, name='chain', out_shape=(pltpu.VMEM((2, N, N), F32...]
where the time goes in v12:
time: 46 us; the launch traced here: 45.8 us
  Pallas kernels  45.2 us (98%)
  between operations  0.64 us (1%)
    pallas_call x1, Pallas kernels, per_device(): pl.pallas_call(kernel, name='chain', out_shape=(pltpu.VMEM((2, N, N), F32...  43.8 us
    pallas_call x1, Pallas kernels, per_device(): pl.pallas_call(finish, name='finish', out_shape=(jax.ShapeDtypeStruct((2,...  1.37 us

profile of v12, /device:TPU:1, one launch (start us, length us, event | category | flops | bytes accessed | tf_op | source)
XLA Modules:
  0.0 45.8 jit_solution(14284987682063819049)
XLA Ops:
  0.6 43.8 %chain.1 = (f32[2,256,256]{2,1,0:T(8,128)S(1)}, f32[8,128]{1,0:T(8,128)S(1)}) custom-call(f32[2,1,256,256]{3,2,1,0:T(8,128)} %t_hbm.1, f32[2,3,1,256,256]{4,3,2,1,0:T(8,128)} %h_hbm.1, s32[1,2]{1,0:T(1,128)} %bitcast.1), custom_call_target="tpu_custom_call" | custom-call | tf_op jit(solution)/shard_map/chain/pallas_call | solution.py:436
  44.5 1.4 %finish.1 = (f32[2,1,256,256]{3,2,1,0:T(8,128)}, f32[2,3]{1,0:T(2,128)}) custom-call(f32[2,256,256]{2,1,0:T(8,128)S(1)} %get-tuple-element.4.lefts, f32[8,128]{1,0:T(8,128)S(1)} %get-tuple-element.5.sums_ref), custom_call_target="tpu_custom_call" | custom-call | tf_op jit(solution)/shard_map/finish/pallas_call | solution.py:469

commit v13 on v12

--- a/solution.py
+++ b/solution.py
@@ -16,7 +16,7 @@
 QUARTER = N // 4
 BASE = 104
 CUTS = ((0, BASE), (BASE, N - 2 * BASE), (N - BASE, BASE))
-SIZES = ((64,), (64,))
+SIZES = ((40, 24), (40, 24))
 PARTS = [(half, sum(sizes[:k]), sizes[k]) for half, sizes in enumerate(SIZES) for k in range(len(sizes))]
 TERMS = 3
 NN = (((1,), (0,)), ((), ()))

time: 46 us -> 45.9 us (level)
  no operation moved by 1% of the time
where the time goes in v13:
time: 45.9 us; the launch traced here: 45.8 us
  Pallas kernels  45.1 us (98%)
  between operations  0.64 us (1%)
    pallas_call x1, Pallas kernels, per_device(): pl.pallas_call(kernel, name='chain', out_shape=(pltpu.VMEM((2, N, N), F32...  43.8 us
    pallas_call x1, Pallas kernels, per_device(): pl.pallas_call(finish, name='finish', out_shape=(jax.ShapeDtypeStruct((2,...  1.37 us

profile of v13, /device:TPU:1, one launch (start us, length us, event | category | flops | bytes accessed | tf_op | source)
XLA Modules:
  0.0 45.8 jit_solution(10596200456451452186)
XLA Ops:
  0.6 43.8 %chain.1 = (f32[2,256,256]{2,1,0:T(8,128)S(1)}, f32[8,128]{1,0:T(8,128)S(1)}) custom-call(f32[2,1,256,256]{3,2,1,0:T(8,128)} %t_hbm.1, f32[2,3,1,256,256]{4,3,2,1,0:T(8,128)} %h_hbm.1, s32[1,2]{1,0:T(1,128)} %bitcast.1), custom_call_target="tpu_custom_call" | custom-call | tf_op jit(solution)/shard_map/chain/pallas_call | solution.py:436
  44.4 1.4 %finish.1 = (f32[2,1,256,256]{3,2,1,0:T(8,128)}, f32[2,3]{1,0:T(2,128)}) custom-call(f32[2,256,256]{2,1,0:T(8,128)S(1)} %get-tuple-element.4.lefts, f32[8,128]{1,0:T(8,128)S(1)} %get-tuple-element.5.sums_ref), custom_call_target="tpu_custom_call" | custom-call | tf_op jit(solution)/shard_map/finish/pallas_call | solution.py:469
